TPU v7x, 32 devices: a whole 2x2x4 slice. The times are simulated.
32 devices in a mesh: gx: 8 (over z, x), gy: 2 (over y), gz: 2 (over core).
Axes of the slice: x: 2, y: 2, z: 4, core: 2. Of those that a mesh axis runs over, the one named last changes fastest.
Arguments:
- state_field: float32 [128, 5, 32, 256], P('gx', None, 'gy', 'gz'), may hold values from -6 to 6
- source: float32 [128, 5, 32, 256], P('gx', None, 'gy', 'gz'), may hold values from -6 to 6
- fluid_mask: int32 [128, 32, 256], P('gx', 'gy', 'gz'), may hold values 0 or 1
- cell_kind: int32 [128, 32, 256], P('gx', 'gy', 'gz'), may hold values from 0 to 2
- boundary_side_number: int32 [128, 32, 256], P('gx', 'gy', 'gz'), may hold values from 0 to 11
- center_matrix: float32 [5, 5], replicated, may hold values from -2.5 to 2.5
- flux_jacobian_blocks: float32 [6, 5, 5], replicated, may hold values from -1 to 1
- wall_matrix: float32 [5, 5], replicated, may hold values from -2.5 to 2.5
- diag_inverse: float32 [128, 5, 5, 32, 256], P('gx', None, None, 'gy', 'gz'), may hold values from -0.01 to 0.1
- lower_coupling: float32 [5, 5], replicated, may hold values from -10 to 10
- upper_neighbour_block: float32 [5, 5], replicated, may hold values from -10 to 10
Outputs:
- update: float32 [128, 5, 32, 256], P('gx', None, 'gy', 'gz')
- residual: float32 [128, 5, 32, 256], P('gx', None, 'gy', 'gz')
Inputs may be any that keep to these rules, and one draw needn't show every extreme that they name: `boundary_side_number`: values 0 to 5 name the face of a cell that is a wall (lower x, upper x, lower y, upper y, lower z, upper z); 6 or more: no wall face. `cell_kind`: 0 full cell, 1 cut cell, 2 small cut cell.
All inputs are finite; a program needn't handle non-finite values. No bound on the sum of `fluid_mask` on one device may be relied on, other than what follows from the above.
Results may differ from a plain program's by a relative error of at most 0.00018.
Values sent between devices are 32-bit elements; how exact they have to be, the bound alone decides.
No kernel may reach another device: no remote copies, remote signals or barrier semaphores. Data moves between devices by JAX's collectives and lax.ppermute only.
A program may use at most 64 MiB of HBM per device.

v0:
```python
import jax
import jax.numpy as jnp
from jax import lax
from jax.sharding import PartitionSpec as P


def with_halo(block, sides, width):
    for axis, dim in sides:
        count = lax.axis_size(axis)
        forward = [(i, i + 1) for i in range(count - 1)]
        backward = [(target, source) for source, target in forward]
        low = lax.ppermute(
            lax.slice_in_dim(block, block.shape[dim] - width, None, axis=dim), axis, forward
        )
        high = lax.ppermute(lax.slice_in_dim(block, 0, width, axis=dim), axis, backward)
        block = jnp.concatenate([low, block, high], axis=dim)
    return block


def const_apply(matrix, vector):
    return jnp.einsum("ab,...byz->...ayz", matrix, vector, precision=lax.Precision.HIGHEST)


def couple(matrix, transfer):
    return jnp.einsum("ab,bcyz->acyz", matrix, transfer, precision=lax.Precision.HIGHEST)


def volume_operator(blocks, vector):
    return jnp.sum(blocks * vector[..., None, :, :, :], axis=-3)


def cell_product(left, right):
    return jnp.sum(left[:, :, None] * right[None], axis=1)


def flux_residual(
    state_field,
    padded,
    source,
    fluid,
    cell_kind,
    boundary_side_number,
    center_matrix,
    flux_jacobian_blocks,
    wall_matrix,
):
    neighbours = [
        padded[:-2, :, 1:-1, 1:-1],
        padded[2:, :, 1:-1, 1:-1],
        padded[1:-1, :, :-2, 1:-1],
        padded[1:-1, :, 2:, 1:-1],
        padded[1:-1, :, 1:-1, :-2],
        padded[1:-1, :, 1:-1, 2:],
    ]
    walled = const_apply(wall_matrix, state_field)
    flux = const_apply(center_matrix, state_field)
    for facing in range(6):
        at_wall = (boundary_side_number == facing)[:, None]
        flux = flux + jnp.where(
            at_wall, walled, const_apply(flux_jacobian_blocks[facing], neighbours[facing])
        )
    weight = jnp.where(cell_kind == 0, 1.0, jnp.where(cell_kind == 1, 2.0, 4.0)).astype(jnp.float32)
    return fluid[:, None] * (source - flux) * weight[:, None]


def pack_maps(transfer, offset):
    comps = offset.shape[0]
    columns = offset.shape[1] * offset.shape[2]
    packed = jnp.concatenate(
        [transfer.reshape(comps * comps, columns), offset.reshape(comps, columns)], axis=0
    )
    return packed[None]


def column_chain(spread, comps, backwards):
    groups = spread.shape[0]
    columns = spread.shape[2]
    matrices = spread[:, : comps * comps].reshape(groups, comps, comps, columns)
    offsets = spread[:, comps * comps :]

    def chain_step(carry, inputs):
        matrix, shift_term = inputs
        following = jnp.sum(matrix * carry[None, :, :], axis=1) + shift_term
        return (following, carry)

    start = jnp.zeros((comps, columns), jnp.float32)
    final, incoming = lax.scan(chain_step, start, (matrices, offsets), reverse=backwards)
    return incoming


def carry_east(transfer, offset):
    spread = lax.all_to_all(
        pack_maps(transfer, offset), "gx", split_axis=2, concat_axis=0, tiled=True
    )
    incoming = column_chain(spread, offset.shape[0], False)
    returned = lax.all_to_all(incoming, "gx", split_axis=0, concat_axis=2, tiled=True)
    return returned.reshape(offset.shape)


def carry_west(transfer, offset):
    spread = lax.all_to_all(
        pack_maps(transfer, offset), "gx", split_axis=2, concat_axis=0, tiled=True
    )
    incoming = column_chain(spread, offset.shape[0], True)
    returned = lax.all_to_all(incoming, "gx", split_axis=0, concat_axis=2, tiled=True)
    return returned.reshape(offset.shape)


def on_device(
    state_field,
    source,
    fluid_mask,
    cell_kind,
    boundary_side_number,
    center_matrix,
    flux_jacobian_blocks,
    wall_matrix,
    diag_inverse,
    lower_coupling,
    upper_neighbour_block,
):
    fluid = fluid_mask.astype(jnp.float32)
    masked = state_field * fluid[:, None]
    padded = with_halo(masked, (("gx", 0), ("gy", 2), ("gz", 3)), 1)
    residual = flux_residual(
        state_field,
        padded,
        source,
        fluid,
        cell_kind,
        boundary_side_number,
        center_matrix,
        flux_jacobian_blocks,
        wall_matrix,
    )
    comps = state_field.shape[1]
    plane_shape = (comps, state_field.shape[2], state_field.shape[3])
    zeroed = jnp.zeros(plane_shape, jnp.float32)
    identity = jnp.broadcast_to(
        jnp.eye(comps, dtype=jnp.float32)[:, :, None, None], (comps, comps) + plane_shape[1:]
    )

    def forward_map(carry, inputs):
        value, transfer = carry
        blocks, term = inputs
        value = volume_operator(blocks, term + const_apply(lower_coupling, value))
        transfer = cell_product(blocks, couple(lower_coupling, transfer))
        return ((value, transfer), None)

    def forward(carry, inputs):
        blocks, term = inputs
        carry = volume_operator(blocks, term + const_apply(lower_coupling, carry))
        return (carry, carry)

    (offset, transfer), unused = lax.scan(forward_map, (zeroed, identity), (diag_inverse, residual))
    incoming = carry_east(transfer, offset)
    final, swept = lax.scan(forward, incoming, (diag_inverse, residual))

    def backward_map(carry, inputs):
        value, transfer = carry
        blocks, term = inputs
        value = term - volume_operator(blocks, const_apply(upper_neighbour_block, value))
        transfer = -cell_product(blocks, couple(upper_neighbour_block, transfer))
        return ((value, transfer), None)

    def backward(carry, inputs):
        blocks, value = inputs
        carry = value - volume_operator(blocks, const_apply(upper_neighbour_block, carry))
        return (carry, carry)

    (offset, transfer), unused = lax.scan(
        backward_map, (zeroed, identity), (diag_inverse, swept), reverse=True
    )
    incoming = carry_west(transfer, offset)
    final, update = lax.scan(backward, incoming, (diag_inverse, swept), reverse=True)
    return (update, residual)


def solution(mesh):
    in_specs = (
        P("gx", None, "gy", "gz"),
        P("gx", None, "gy", "gz"),
        P("gx", "gy", "gz"),
        P("gx", "gy", "gz"),
        P("gx", "gy", "gz"),
        P(),
        P(),
        P(),
        P("gx", None, None, "gy", "gz"),
        P(),
        P(),
    )
    out_specs = (P("gx", None, "gy", "gz"), P("gx", None, "gy", "gz"))
    return jax.shard_map(
        on_device, mesh=mesh, in_specs=in_specs, out_specs=out_specs, check_vma=False
    )
```

profile of v0, /device:TPU:0, one launch (start us, length us, event | category | flops | bytes accessed | tf_op | source)
XLA Modules:
  0.0 266.1 jit_solution(13816744103888163784)
XLA Ops:
  3.2 5.0 %collective-permute-start = (f32[1,5,16,128]{3,1,2,0:T(8,128)S(1)}, f32[1,5,16,128]{3,1,2,0:T(8,128)S(1)}, u32[]{:S(2)}, u32[]{:S(2)}) collective-permute-start(f32[1,5,16,128]{3,1,2,0:T(8,128)S(1)} %get-tuple-element.649), channel_id=1, source_target_pairs={{0,4},{4,8},{8,12},{12,16},{16,20},{20,24},{24,28},{1,5},{5,9},{9,... | collective-permute-start | bytes 122888 | tf_op jit(solution)/shard_map/ppermute | solution.py:12
  11.5 2.2 fusion.37
  14.4 3.4 %collective-permute-start.2 = (f32[18,5,1,128]{3,1,2,0:T(8,128)S(1)}, f32[18,5,1,128]{3,1,2,0:T(8,128)S(1)}, u32[]{:S(2)}, u32[]{:S(2)}) collective-permute-start(f32[18,5,1,128]{3,1,2,0:T(8,128)S(1)} %get-tuple-element.647), channel_id=1, source_target_pairs={{0,2},{1,3},{4,6},{5,7},{8,10},{9,11},{12,14},{13,15},{16,18},{17,... | collective-permute-start | bytes 138248 | tf_op jit(solution)/shard_map/ppermute | solution.py:12
  19.2 2.1 convolution_select_fusion.2
  21.3 2.8 %collective-permute-done.3 = f32[18,5,1,128]{3,1,2,0:T(8,128)S(1)} collective-permute-done((f32[18,5,1,128]{3,1,2,0:T(8,128)S(1)}, f32[18,5,1,128]{3,1,2,0:T(8,128)S(1)}, u32[]{:S(2)}, u32[]{:S(2)}) %collective-permute-start.3) | collective-permute-done | bytes 46112 | tf_op jit(solution)/shard_map/ppermute | solution.py:15
  26.4 2.6 copy.197
  28.9 1.9 collective-permute-start.4
  33.6 3.0 %convolution_select_fusion = f32[16,16,128,5]{2,3,1,0:T(8,128)} fusion(f32[16,16,128,5]{2,3,1,0:T(8,128)S(1)} %fusion.35, f32[18,5,1,128]{3,1,2,0:T(8,128)} %copy-done.16, f32[1,5,16,128]{3,1,2,0:T(8,128)} %copy-done.6, f32[16,5,16,128]{3,1,2,0:T(8,128)S(1)} %copy_multiply_fusion, f32[1,5,16,128]{3,1,2,0:T(8,128)S(1)} %collective-permute-done, ...), kind=kOutput, calls=%fused_computation.52 | convolution fusion | flops 10581760 | bytes 2126948 | tf_op jit(solution)/shard_map/ab,...byz->...ayz/dot_general | solution.py:21
  36.6 2.2 convolution_select_fusion.1
  38.8 2.8 %copy.198 = f32[18,5,18,1]{3,1,2,0:T(8,128)} copy(f32[18,5,18,1]{2,3,1,0:T(1,128)} %collective-permute-done.4) | data formatting | bytes 12960 | tf_op jit(solution)/shard_map/ppermute | solution.py:12
  41.6 1.7 copy.201
  43.4 2.6 convolution_select_fusion.5
  50.1 28.6 %while.87 = (s32[]{:T(128)}, f32[5,16,128]{2,1,0:T(8,128)S(1)}, f32[5,5,16,128]{3,2,1,0:T(8,128)S(1)}, f32[16,5,5,16,128]{4,3,2,1,0:T(8,128)}, f32[16,5,16,128]{...) while((s32[]{:T(128)}, f32[5,16,128]{2,1,0:T(8,128)S(1)}, f32[5,5,16,128]{3,2,1,0:T(8,128)S(1)}, ...), condition=%wide.region_3.4_spmd, body=%wide.region_0.3_spmd.sunk | while | flops 4249602 | bytes 2130205 | solution.py:155
  80.1 9.3 %reduce = f32[2048,30]{1,0:T(8,128)S(1)} reduce(f32[2048,1,30]{2,1,0:T(1,128)S(1)} %bitcast.220, f32[]{:T(128)} %broadcast.68), dimensions={1}, to_apply=%bitcast.170.reduce_sub_computation | reduce | bytes 491524
  89.4 1.8 reshape.87
  91.2 7.0 %all-to-all-start = ((f32[8,1,7680]{2,1,0:T(1,128)}), f32[8,1,7680]{2,1,0:T(1,128)S(1)}, u32[]{:S(2)}, u32[]{:S(2)}) async-start(f32[8,1,7680]{2,1,0:T(1,128)} %reshape.87), calls=%async_computation | async-start | bytes 491520 | tf_op jit(solution)/shard_map/all_to_all | solution.py:92
  98.1 9.7 %all-to-all-done = f32[8,1,7680]{2,1,0:T(1,128)S(1)} async-done(((f32[8,1,7680]{2,1,0:T(1,128)}), f32[8,1,7680]{2,1,0:T(1,128)S(1)}, u32[]{:S(2)}, u32[]{:S(2)}) %all-to-all-start) | async-done | bytes 245792 | tf_op jit(solution)/shard_map/all_to_all | solution.py:92
  109.0 1.9 reshape.88
  111.9 5.7 %while.90 = (s32[]{:T(128)}, f32[5,256]{1,0:T(8,128)S(1)}, f32[8,5,256]{2,1,0:T(8,128)}, f32[8,5,5,256]{3,0,2,1:T(8,128)S(1)}, f32[8,5,256]{2,0,1:T(8,128)S(1)}, /*index=5*/s32[]{:T(128)}, s32[]{:T(128)}) while((s32[]{:T(128)}, f32[5,256]{1,0:T(8,128)S(1)}, f32[8,5,256]{2,1,0:T(8,128)}, f32[8,5,5,256]{3,0,2,1:T(8,128)S(1)}, ...), condition=%wide.region_6.7_spmd.clone, body=%wide.region_4.6_spmd.clone.sunk | while | flops 14083 | bytes 131679 | solution.py:87
  117.6 3.9 %all-to-all-start.1 = ((f32[8,5,256]{2,1,0:T(8,128)}), f32[8,5,256]{2,1,0:T(8,128)S(1)}, u32[]{:S(2)}, u32[]{:S(2)}) async-start(f32[8,5,256]{2,1,0:T(8,128)} %get-tuple-element.444), calls=%async_computation.1 | async-start | bytes 131072 | tf_op jit(solution)/shard_map/all_to_all | solution.py:96
  121.5 6.9 %all-to-all-done.1 = f32[8,5,256]{2,1,0:T(8,128)S(1)} async-done(((f32[8,5,256]{2,1,0:T(8,128)}), f32[8,5,256]{2,1,0:T(8,128)S(1)}, u32[]{:S(2)}, u32[]{:S(2)}) %all-to-all-start.1) | async-done | bytes 40992 | tf_op jit(solution)/shard_map/all_to_all | solution.py:96
  128.5 19.3 %while.88 = (s32[]{:T(128)}, f32[5,16,128]{2,1,0:T(8,128)S(1)}, f32[16,5,16,128]{3,2,1,0:T(8,128)S(1)}, f32[16,5,5,16,128]{4,3,2,1,0:T(8,128)}, f32[16,5,16,128]...) while((s32[]{:T(128)}, f32[5,16,128]{2,1,0:T(8,128)S(1)}, f32[16,5,16,128]{3,2,1,0:T(8,128)S(1)}, ...), condition=%wide.region_9.10_spmd, body=%wide.region_7.9_spmd.sunk | while | flops 716802 | bytes 573629 | solution.py:157
  147.9 29.2 %while.91 = (s32[]{:T(128)}, f32[5,16,128]{2,1,0:T(8,128)S(1)}, f32[5,5,16,128]{3,2,1,0:T(8,128)S(1)}, f32[16,5,16,128]{3,2,1,0:T(8,128)S(1)}, f32[16,5,5,16,128...) while((s32[]{:T(128)}, f32[5,16,128]{2,1,0:T(8,128)S(1)}, ...), condition=%wide.region_13.14_spmd.clone, body=%wide.region_10.13_spmd.clone.sunk | while | flops 4311044 | bytes 2703683 | solution.py:171
  178.7 9.3 %reduce.2 = f32[2048,30]{1,0:T(8,128)S(1)} reduce(f32[2048,1,30]{2,1,0:T(1,128)S(1)} %bitcast.222, f32[]{:T(128)} %broadcast.68), dimensions={1}, to_apply=%bitcast.172.reduce_sub_computation | reduce | bytes 491524
  188.0 1.8 reshape.89
  189.8 3.4 %all-to-all-start.2 = ((f32[8,1,7680]{2,1,0:T(1,128)}), f32[8,1,7680]{2,1,0:T(1,128)S(1)}, u32[]{:S(2)}, u32[]{:S(2)}) async-start(f32[8,1,7680]{2,1,0:T(1,128)} %reshape.89), calls=%async_computation.2 | async-start | bytes 491520 | tf_op jit(solution)/shard_map/all_to_all | solution.py:101
  193.2 8.0 %all-to-all-done.2 = f32[8,1,7680]{2,1,0:T(1,128)S(1)} async-done(((f32[8,1,7680]{2,1,0:T(1,128)}), f32[8,1,7680]{2,1,0:T(1,128)S(1)}, u32[]{:S(2)}, u32[]{:S(2)}) %all-to-all-start.2) | async-done | bytes 245792 | tf_op jit(solution)/shard_map/all_to_all | solution.py:101
  202.4 1.9 reshape.90
  205.3 5.6 %while.92 = (s32[]{:T(128)}, f32[5,256]{1,0:T(8,128)S(1)}, f32[8,5,256]{2,1,0:T(8,128)}, f32[8,5,5,256]{3,0,2,1:T(8,128)S(1)}, f32[8,5,256]{2,0,1:T(8,128)S(1)}, /*index=5*/s32[]{:T(128)}, s32[]{:T(128)}, s32[]{:T(128)}) while((s32[]{:T(128)}, f32[5,256]{1,0:T(8,128)S(1)}, f32[8,5,256]{2,1,0:T(8,128)}, ...), condition=%wide.region_16.17_spmd.clone, body=%wide.region_14.16_spmd.clone.sunk | while | flops 14084 | bytes 131191 | solution.py:87
  211.0 3.4 %all-to-all-start.3 = ((f32[8,5,256]{2,1,0:T(8,128)}), f32[8,5,256]{2,1,0:T(8,128)S(1)}, u32[]{:S(2)}, u32[]{:S(2)}) async-start(f32[8,5,256]{2,1,0:T(8,128)} %get-tuple-element.448), calls=%async_computation.3 | async-start | bytes 131072 | tf_op jit(solution)/shard_map/all_to_all | solution.py:105
  215.3 5.9 %all-to-all-done.3 = f32[8,5,256]{2,1,0:T(8,128)S(1)} async-done(((f32[8,5,256]{2,1,0:T(8,128)}), f32[8,5,256]{2,1,0:T(8,128)S(1)}, u32[]{:S(2)}, u32[]{:S(2)}) %all-to-all-start.3) | async-done | bytes 40992 | tf_op jit(solution)/shard_map/all_to_all | solution.py:105
  221.3 44.0 %while.89 = (s32[]{:T(128)}, f32[5,16,128]{2,1,0:T(8,128)S(1)}, f32[16,5,16,128]{3,2,1,0:T(8,128)S(1)}, f32[16,5,16,128]{3,2,1,0:T(8,128)}, f32[16,5,5,16,128]{4...) while((s32[]{:T(128)}, f32[5,16,128]{2,1,0:T(8,128)S(1)}, ...), condition=%wide.region_19.20_spmd, body=%wide.region_17.19_spmd.sunk | while | flops 727043 | bytes 696529 | solution.py:175
  (576 shorter events, 154.4 us)
Async XLA Ops:
  0.6 8.8 %copy-start = (f32[5,5]{1,0:T(8,128)S(1)}, f32[5,5]{1,0:T(8,128)}, u32[]{:S(2)}) copy-start(f32[5,5]{1,0:T(8,128)} %param.30) | copy-start | bytes 304
  0.6 8.8 %copy-start.1 = (f32[16,5,16,128]{3,2,1,0:T(8,128)S(1)}, f32[16,5,16,128]{3,2,1,0:T(8,128)}, u32[]{:S(2)}) copy-start(f32[16,5,16,128]{3,2,1,0:T(8,128)} %param.23) | copy-start | bytes 1966084
  1.6 9.1 %copy-start.11 = (f32[16,16,128]{2,1,0:T(8,128)}, f32[16,16,128]{2,1,0:T(8,128)S(1)}, u32[]{:S(2)}) copy-start(f32[16,16,128]{2,1,0:T(8,128)S(1)} %convert_element_type.13) | copy-start | bytes 393220
  3.1 7.6 %copy-start.24 = (s32[16,16,128]{2,1,0:T(8,128)S(1)}, s32[16,16,128]{2,1,0:T(8,128)}, u32[]{:S(2)}) copy-start(s32[16,16,128]{2,1,0:T(8,128)} %param.27) | copy-start | bytes 393220
  3.1 8.4 %copy-start.26 = (f32[6,5,5]{2,0,1:T(8,128)S(1)}, f32[6,5,5]{2,0,1:T(8,128)}, u32[]{:S(2)}) copy-start(f32[6,5,5]{2,0,1:T(8,128)} %param.29) | copy-start | bytes 1804
  3.1 8.4 %copy-start.27 = (f32[5,5]{1,0:T(8,128)S(1)}, f32[5,5]{1,0:T(8,128)}, u32[]{:S(2)}) copy-start(f32[5,5]{1,0:T(8,128)} %param.28) | copy-start | bytes 304
  3.2 11.2 %collective-permute-start = (f32[1,5,16,128]{3,1,2,0:T(8,128)S(1)}, f32[1,5,16,128]{3,1,2,0:T(8,128)S(1)}, u32[]{:S(2)}, u32[]{:S(2)}) collective-permute-start(f32[1,5,16,128]{3,1,2,0:T(8,128)S(1)} %get-tuple-element.649), channel_id=1, source_target_pairs={{0,4},{4,8},{8,12},{12,16},{16,20},{20,24},{24,28},{1,5},{5,9},{9,... | collective-permute-start | bytes 122888 | tf_op jit(solution)/shard_map/ppermute | solution.py:12
  8.2 6.2 %collective-permute-start.1 = (f32[1,5,16,128]{3,1,2,0:T(8,128)S(1)}, f32[1,5,16,128]{3,1,2,0:T(8,128)S(1)}, u32[]{:S(2)}, u32[]{:S(2)}) collective-permute-start(f32[1,5,16,128]{3,1,2,0:T(8,128)S(1)} %get-tuple-element.650), channel_id=1, source_target_pairs={{4,0},{8,4},{12,8},{16,12},{20,16},{24,20},{28,24},{5,1},{9,5},{13... | collective-permute-start | bytes 122888 | tf_op jit(solution)/shard_map/ppermute | solution.py:15
  10.7 3.0 %copy-start.25 = (s32[16,16,128]{2,1,0:T(8,128)S(1)}, s32[16,16,128]{2,1,0:T(8,128)}, u32[]{:S(2)}) copy-start(s32[16,16,128]{2,1,0:T(8,128)} %param.26) | copy-start | bytes 393220
  14.4 9.7 %copy-start.6 = (f32[1,5,16,128]{3,1,2,0:T(8,128)}, f32[1,5,16,128]{3,1,2,0:T(8,128)S(1)}, u32[]{:S(2)}) copy-start(f32[1,5,16,128]{3,1,2,0:T(8,128)S(1)} %collective-permute-done.1) | copy-start | bytes 122884
  14.4 6.9 %collective-permute-start.2 = (f32[18,5,1,128]{3,1,2,0:T(8,128)S(1)}, f32[18,5,1,128]{3,1,2,0:T(8,128)S(1)}, u32[]{:S(2)}, u32[]{:S(2)}) collective-permute-start(f32[18,5,1,128]{3,1,2,0:T(8,128)S(1)} %get-tuple-element.647), channel_id=1, source_target_pairs={{0,2},{1,3},{4,6},{5,7},{8,10},{9,11},{12,14},{13,15},{16,18},{17,... | collective-permute-start | bytes 138248 | tf_op jit(solution)/shard_map/ppermute | solution.py:12
  17.9 6.2 %collective-permute-start.3 = (f32[18,5,1,128]{3,1,2,0:T(8,128)S(1)}, f32[18,5,1,128]{3,1,2,0:T(8,128)S(1)}, u32[]{:S(2)}, u32[]{:S(2)}) collective-permute-start(f32[18,5,1,128]{3,1,2,0:T(8,128)S(1)} %get-tuple-element.648), channel_id=1, source_target_pairs={{2,0},{3,1},{6,4},{7,5},{10,8},{11,9},{14,12},{15,13},{18,16},{19,... | collective-permute-start | bytes 138248 | tf_op jit(solution)/shard_map/ppermute | solution.py:15
  21.3 2.8 %copy-start.13 = (f32[18,5,1,128]{3,1,2,0:T(8,128)}, f32[18,5,1,128]{3,1,2,0:T(8,128)S(1)}, u32[]{:S(2)}) copy-start(f32[18,5,1,128]{3,1,2,0:T(8,128)S(1)} %collective-permute-done.2) | copy-start | bytes 138244
  28.9 9.9 %collective-permute-start.4 = (f32[18,5,18,1]{2,3,1,0:T(1,128)}, f32[18,5,18,1]{2,3,1,0:T(1,128)}, u32[]{:S(2)}, u32[]{:S(2)}) collective-permute-start(f32[18,5,18,1]{2,3,1,0:T(1,128)} %copy.197), channel_id=1, source_target_pairs={{0,1},{2,3},{4,5},{6,7},{8,9},{10,11},{12,13},{14,15},{16,17},{18,... | collective-permute-start | bytes 19448 | tf_op jit(solution)/shard_map/ppermute | solution.py:12
  32.1 9.6 %collective-permute-start.5 = (f32[18,5,18,1]{2,3,1,0:T(1,128)}, f32[18,5,18,1]{2,3,1,0:T(1,128)}, u32[]{:S(2)}, u32[]{:S(2)}) collective-permute-start(f32[18,5,18,1]{2,3,1,0:T(1,128)} %copy.200), channel_id=1, source_target_pairs={{1,0},{3,2},{5,4},{7,6},{9,8},{11,10},{13,12},{15,14},{17,16},{19,... | collective-permute-start | bytes 19448 | tf_op jit(solution)/shard_map/ppermute | solution.py:15
  33.6 3.1 %copy-start.7 = (f32[1,5,16,128]{3,1,2,0:T(8,128)S(1)}, f32[1,5,16,128]{3,1,2,0:T(8,128)}, u32[]{:S(2)}) copy-start(f32[1,5,16,128]{3,1,2,0:T(8,128)} %copy-done.6) | copy-start | bytes 122884
  33.6 3.1 %copy-start.14 = (f32[18,5,1,128]{3,1,2,0:T(8,128)S(1)}, f32[18,5,1,128]{3,1,2,0:T(8,128)}, u32[]{:S(2)}) copy-start(f32[18,5,1,128]{3,1,2,0:T(8,128)} %copy-done.13) | copy-start | bytes 138244
  33.6 3.1 %copy-start.23 = (pred[16,16,128]{2,1,0:T(8,128)(4,1)S(1)}, pred[16,16,128]{2,1,0:T(8,128)(4,1)}, u32[]{:S(2)}) copy-start(pred[16,16,128]{2,1,0:T(8,128)(4,1)} %get-tuple-element.653) | copy-start | bytes 98308
  43.4 2.7 %copy-start.8 = (f32[1,5,16,128]{3,1,2,0:T(8,128)S(1)}, f32[1,5,16,128]{3,1,2,0:T(8,128)}, u32[]{:S(2)}) copy-start(f32[1,5,16,128]{3,1,2,0:T(8,128)} %copy-done.6) | copy-start | bytes 122884
  43.4 2.7 %copy-start.15 = (f32[18,5,1,128]{3,1,2,0:T(8,128)S(1)}, f32[18,5,1,128]{3,1,2,0:T(8,128)}, u32[]{:S(2)}) copy-start(f32[18,5,1,128]{3,1,2,0:T(8,128)} %copy-done.13) | copy-start | bytes 138244
  43.4 2.7 %copy-start.17 = (f32[18,5,1,128]{3,1,2,0:T(8,128)S(1)}, f32[18,5,1,128]{3,1,2,0:T(8,128)}, u32[]{:S(2)}) copy-start(f32[18,5,1,128]{3,1,2,0:T(8,128)} %copy-done.16) | copy-start | bytes 138244
  43.4 2.7 %copy-start.22 = (pred[16,16,128]{2,1,0:T(8,128)(4,1)S(1)}, pred[16,16,128]{2,1,0:T(8,128)(4,1)}, u32[]{:S(2)}) copy-start(pred[16,16,128]{2,1,0:T(8,128)(4,1)} %get-tuple-element.655) | copy-start | bytes 98308
  43.4 4.3 %copy-start.10 = (f32[16,5,16,128]{3,2,1,0:T(8,128)S(1)}, f32[16,5,16,128]{3,2,1,0:T(8,128)}, u32[]{:S(2)}) copy-start(f32[16,5,16,128]{3,2,1,0:T(8,128)} %param.24) | copy-start | bytes 1966084
  46.1 1.8 copy-start.4
  46.1 2.1 copy-start.5
  46.1 2.1 copy-start.12
  46.2 2.2 copy-start.21
  91.2 16.6 %all-to-all-start = ((f32[8,1,7680]{2,1,0:T(1,128)}), f32[8,1,7680]{2,1,0:T(1,128)S(1)}, u32[]{:S(2)}, u32[]{:S(2)}) async-start(f32[8,1,7680]{2,1,0:T(1,128)} %reshape.87), calls=%async_computation | async-start | bytes 491520 | tf_op jit(solution)/shard_map/all_to_all | solution.py:92
  117.6 10.8 %all-to-all-start.1 = ((f32[8,5,256]{2,1,0:T(8,128)}), f32[8,5,256]{2,1,0:T(8,128)S(1)}, u32[]{:S(2)}, u32[]{:S(2)}) async-start(f32[8,5,256]{2,1,0:T(8,128)} %get-tuple-element.444), calls=%async_computation.1 | async-start | bytes 131072 | tf_op jit(solution)/shard_map/all_to_all | solution.py:96
  128.5 19.4 %copy-start.19 = (f32[5,5]{1,0:T(8,128)S(1)}, f32[5,5]{1,0:T(8,128)}, u32[]{:S(2)}) copy-start(f32[5,5]{1,0:T(8,128)} %param.33) | copy-start | bytes 304
  189.8 11.5 %all-to-all-start.2 = ((f32[8,1,7680]{2,1,0:T(1,128)}), f32[8,1,7680]{2,1,0:T(1,128)S(1)}, u32[]{:S(2)}, u32[]{:S(2)}) async-start(f32[8,1,7680]{2,1,0:T(1,128)} %reshape.89), calls=%async_computation.2 | async-start | bytes 491520 | tf_op jit(solution)/shard_map/all_to_all | solution.py:101
  211.0 10.2 %all-to-all-start.3 = ((f32[8,5,256]{2,1,0:T(8,128)}), f32[8,5,256]{2,1,0:T(8,128)S(1)}, u32[]{:S(2)}, u32[]{:S(2)}) async-start(f32[8,5,256]{2,1,0:T(8,128)} %get-tuple-element.448), calls=%async_computation.3 | async-start | bytes 131072 | tf_op jit(solution)/shard_map/all_to_all | solution.py:105
  (6 other events, 7.4 us)
where the time goes:
time: 271 us; the launch traced here: 266 us
  other arithmetic  125 us (46%)
  matrix products  42.5 us (16%)
  waiting for transfers between devices  33.3 us (12%)
  starting transfers between devices  32 us (12%)
  local copies, waits for them, and re-layouts  28.1 us (10%)
  loops' own time  3.88 us (1%)
    reduce_sum x64, other arithmetic, volume_operator(): return jnp.sum(blocks * vector[..., None, :, :, :], axis=-3)  61.3 us
    dot_general x72, matrix products, const_apply(): jnp.einsum('ab,...byz->...ayz', matrix, vector, precision=lax.Precision.H...  28.5 us
    unnamed x5, other arithmetic  18.6 us
    dot_general x32, matrix products, couple(): jnp.einsum('ab,bcyz->acyz', matrix, transfer, precision=lax.Precision.HIG...  14.1 us
    dynamic_update_slice x16, other arithmetic, on_device(): final, swept = lax.scan(forward, incoming, (diag_inverse, residual))  12.7 us
    sub x16, other arithmetic, backward(): value - volume_operator(blocks, const_apply(upper_neighbour_block, carry))  12.6 us
    unnamed x68, local copies, waits for them, and re-layouts  11.9 us
    ppermute x3, starting transfers between devices, with_halo(): lax.ppermute(lax.slice_in_dim(block, block.shape[dim] - width, None, axis...  10.3 us
  transfers between devices with their start and end apart: 10, of which 5 were waited for; matrix products, arithmetic and copies ran while one was open for 6% of the time, Pallas kernels for 0%

commit v1 on v0

--- a/solution.py
+++ b/solution.py
@@ -89,8 +89,11 @@
 
 
 def carry_east(transfer, offset):
-    spread = lax.all_to_all(
-        pack_maps(transfer, offset), "gx", split_axis=2, concat_axis=0, tiled=True
+    spread = jnp.concatenate(
+        lax.all_to_all(
+            jnp.stack(jnp.split(pack_maps(transfer, offset), lax.psum(1, "gx"), 2)), "gx", 0, 0
+        ),
+        axis=0,
     )
     incoming = column_chain(spread, offset.shape[0], False)
     returned = lax.all_to_all(incoming, "gx", split_axis=0, concat_axis=2, tiled=True)

time: 271 us -> 260 us (0.959)
  other arithmetic: 125 us -> 115 us
    unnamed x5 -> x4, other arithmetic: 18.6 us -> 9.37 us
    unnamed x68 -> x73, local copies, waits for them, and re-layouts: 11.9 us -> 12.6 us
  transfers between devices with their start and end apart: 10 -> 10, of which waited for: 5 -> 5; matrix products, arithmetic and copies ran while one was open for 6% -> 7% of each run, Pallas kernels for 0% -> 0%
where the time goes in v1:
time: 260 us; the launch traced here: 256 us
  other arithmetic  115 us (44%)
  matrix products  42.5 us (16%)
  waiting for transfers between devices  33.3 us (13%)
  starting transfers between devices  32 us (12%)
  local copies, waits for them, and re-layouts  28.6 us (11%)
  loops' own time  3.66 us (1%)
    reduce_sum x64, other arithmetic, volume_operator(): return jnp.sum(blocks * vector[..., None, :, :, :], axis=-3)  61.3 us
    dot_general x72, matrix products, const_apply(): jnp.einsum('ab,...byz->...ayz', matrix, vector, precision=lax.Precision.H...  28.4 us
    dot_general x32, matrix products, couple(): jnp.einsum('ab,bcyz->acyz', matrix, transfer, precision=lax.Precision.HIG...  14.1 us
    dynamic_update_slice x16, other arithmetic, on_device(): final, swept = lax.scan(forward, incoming, (diag_inverse, residual))  12.7 us
    unnamed x73, local copies, waits for them, and re-layouts  12.6 us
    sub x16, other arithmetic, backward(): value - volume_operator(blocks, const_apply(upper_neighbour_block, carry))  12.6 us
    ppermute x3, starting transfers between devices, with_halo(): lax.ppermute(lax.slice_in_dim(block, block.shape[dim] - width, None, axis...  10.3 us
    all_to_all x1, waiting for transfers between devices, carry_east(): lax.all_to_all(jnp.stack(jnp.split(pack_maps(transfer, offset), lax.psum(...  9.68 us
  transfers between devices with their start and end apart: 10, of which 5 were waited for; matrix products, arithmetic and copies ran while one was open for 7% of the time, Pallas kernels for 0%

profile of v1, /device:TPU:0, one launch (start us, length us, event | category | flops | bytes accessed | tf_op | source)
XLA Modules:
  0.0 255.9 jit_solution(9902694316995722756)
XLA Ops:
  3.2 5.0 %collective-permute-start = (f32[1,5,16,128]{3,1,2,0:T(8,128)S(1)}, f32[1,5,16,128]{3,1,2,0:T(8,128)S(1)}, u32[]{:S(2)}, u32[]{:S(2)}) collective-permute-start(f32[1,5,16,128]{3,1,2,0:T(8,128)S(1)} %get-tuple-element.649), channel_id=1, source_target_pairs={{0,4},{4,8},{8,12},{12,16},{16,20},{20,24},{24,28},{1,5},{5,9},{9,... | collective-permute-start | bytes 122888 | tf_op jit(solution)/shard_map/ppermute | solution.py:12
  11.5 2.2 fusion.37
  14.5 3.4 %collective-permute-start.2 = (f32[18,5,1,128]{3,1,2,0:T(8,128)S(1)}, f32[18,5,1,128]{3,1,2,0:T(8,128)S(1)}, u32[]{:S(2)}, u32[]{:S(2)}) collective-permute-start(f32[18,5,1,128]{3,1,2,0:T(8,128)S(1)} %get-tuple-element.647), channel_id=1, source_target_pairs={{0,2},{1,3},{4,6},{5,7},{8,10},{9,11},{12,14},{13,15},{16,18},{17,... | collective-permute-start | bytes 138248 | tf_op jit(solution)/shard_map/ppermute | solution.py:12
  19.2 2.1 convolution_select_fusion.2
  21.3 2.8 %collective-permute-done.3 = f32[18,5,1,128]{3,1,2,0:T(8,128)S(1)} collective-permute-done((f32[18,5,1,128]{3,1,2,0:T(8,128)S(1)}, f32[18,5,1,128]{3,1,2,0:T(8,128)S(1)}, u32[]{:S(2)}, u32[]{:S(2)}) %collective-permute-start.3) | collective-permute-done | bytes 46112 | tf_op jit(solution)/shard_map/ppermute | solution.py:15
  24.9 1.5 fusion.78
  26.4 2.6 copy.207
  28.9 1.9 collective-permute-start.4
  33.6 3.0 %convolution_select_fusion = f32[16,16,128,5]{2,3,1,0:T(8,128)} fusion(f32[16,16,128,5]{2,3,1,0:T(8,128)S(1)} %fusion.35, f32[18,5,1,128]{3,1,2,0:T(8,128)} %copy-done.16, f32[1,5,16,128]{3,1,2,0:T(8,128)} %copy-done.6, f32[16,5,16,128]{3,1,2,0:T(8,128)S(1)} %copy_multiply_fusion, f32[1,5,16,128]{3,1,2,0:T(8,128)S(1)} %collective-permute-done, ...), kind=kOutput, calls=%fused_computation.52 | convolution fusion | flops 10581760 | bytes 2126948 | tf_op jit(solution)/shard_map/ab,...byz->...ayz/dot_general | solution.py:21
  36.6 2.2 convolution_select_fusion.1
  38.8 2.8 %copy.208 = f32[18,5,18,1]{3,1,2,0:T(8,128)} copy(f32[18,5,18,1]{2,3,1,0:T(1,128)} %collective-permute-done.4) | data formatting | bytes 12960 | tf_op jit(solution)/shard_map/ppermute | solution.py:12
  41.6 1.7 copy.211
  43.4 2.6 %convolution_select_fusion.5 = f32[16,16,128,5]{2,3,1,0:T(8,128)S(1)} fusion(f32[16,16,128,5]{2,3,1,0:T(8,128)S(1)} %fusion.35, f32[18,5,18,1]{3,1,2,0:T(8,128)} %copy.208, f32[18,5,1,128]{3,1,2,0:T(8,128)} %copy-done.16, f32[18,5,1,128]{3,1,2,0:T(8,128)} %copy-done.13, f32[1,5,16,128]{3,1,2,0:T(8,128)} %copy-done.6, ...), kind=kOutput, calls=%fused_computation.57 | convolution fusion | flops 10813440 | bytes 2179508 | tf_op jit(solution)/shard_map/ab,...byz->...ayz/dot_general | solution.py:21
  46.1 1.5 convolution_select_fusion.4
  48.3 1.7 fusion.34
  50.1 28.4 %while.87 = (s32[]{:T(128)}, f32[5,16,128]{2,1,0:T(8,128)S(1)}, f32[5,5,16,128]{3,2,1,0:T(8,128)S(1)}, f32[16,5,5,16,128]{4,3,2,1,0:T(8,128)}, f32[16,5,16,128]{...) while((s32[]{:T(128)}, f32[5,16,128]{2,1,0:T(8,128)S(1)}, f32[5,5,16,128]{3,2,1,0:T(8,128)S(1)}, ...), condition=%wide.region_3.4_spmd, body=%wide.region_0.3_spmd.sunk | while | flops 4249602 | bytes 2130205 | solution.py:158
  83.8 7.0 %all-to-all-start = ((f32[8,1,30,256]{3,1,2,0:T(1,128)}), f32[8,1,30,256]{3,1,2,0:T(1,128)S(1)}, u32[]{:S(2)}, u32[]{:S(2)}) async-start(f32[8,1,30,256]{3,1,2,0:T(1,128)} %fusion.61), calls=%async_computation | async-start | bytes 491520 | tf_op jit(solution)/shard_map/all_to_all | solution.py:93
  90.8 9.7 %all-to-all-done = f32[8,1,30,256]{3,1,2,0:T(1,128)S(1)} async-done(((f32[8,1,30,256]{3,1,2,0:T(1,128)}), f32[8,1,30,256]{3,1,2,0:T(1,128)S(1)}, u32[]{:S(2)}, u32[]{:S(2)}) %all-to-all-start) | async-done | bytes 245792 | tf_op jit(solution)/shard_map/all_to_all | solution.py:93
  101.1 5.7 %while.90 = (s32[]{:T(128)}, f32[5,256]{1,0:T(8,128)S(1)}, f32[8,5,256]{2,1,0:T(8,128)}, f32[8,5,5,256]{3,0,2,1:T(8,128)S(1)}, f32[8,5,256]{2,0,1:T(8,128)S(1)}, /*index=5*/s32[]{:T(128)}, s32[]{:T(128)}) while((s32[]{:T(128)}, f32[5,256]{1,0:T(8,128)S(1)}, f32[8,5,256]{2,1,0:T(8,128)}, f32[8,5,5,256]{3,0,2,1:T(8,128)S(1)}, ...), condition=%wide.region_6.7_spmd.clone, body=%wide.region_4.6_spmd.clone.sunk | while | flops 14083 | bytes 131679 | solution.py:87
  106.8 3.9 %all-to-all-start.1 = ((f32[8,5,256]{2,1,0:T(8,128)}), f32[8,5,256]{2,1,0:T(8,128)S(1)}, u32[]{:S(2)}, u32[]{:S(2)}) async-start(f32[8,5,256]{2,1,0:T(8,128)} %get-tuple-element.444), calls=%async_computation.1 | async-start | bytes 131072 | tf_op jit(solution)/shard_map/all_to_all | solution.py:99
  110.7 6.9 %all-to-all-done.1 = f32[8,5,256]{2,1,0:T(8,128)S(1)} async-done(((f32[8,5,256]{2,1,0:T(8,128)}), f32[8,5,256]{2,1,0:T(8,128)S(1)}, u32[]{:S(2)}, u32[]{:S(2)}) %all-to-all-start.1) | async-done | bytes 40992 | tf_op jit(solution)/shard_map/all_to_all | solution.py:99
  117.7 19.3 %while.88 = (s32[]{:T(128)}, f32[5,16,128]{2,1,0:T(8,128)S(1)}, f32[16,5,16,128]{3,2,1,0:T(8,128)S(1)}, f32[16,5,5,16,128]{4,3,2,1,0:T(8,128)}, f32[16,5,16,128]...) while((s32[]{:T(128)}, f32[5,16,128]{2,1,0:T(8,128)S(1)}, f32[16,5,16,128]{3,2,1,0:T(8,128)S(1)}, ...), condition=%wide.region_9.10_spmd, body=%wide.region_7.9_spmd.sunk | while | flops 716802 | bytes 573629 | solution.py:160
  137.1 29.2 %while.91 = (s32[]{:T(128)}, f32[5,16,128]{2,1,0:T(8,128)S(1)}, f32[5,5,16,128]{3,2,1,0:T(8,128)S(1)}, f32[16,5,16,128]{3,2,1,0:T(8,128)S(1)}, f32[16,5,5,16,128...) while((s32[]{:T(128)}, f32[5,16,128]{2,1,0:T(8,128)S(1)}, ...), condition=%wide.region_13.14_spmd.clone, body=%wide.region_10.13_spmd.clone.sunk | while | flops 4311044 | bytes 2703683 | solution.py:174
  168.4 9.4 %reduce = f32[2048,30]{1,0:T(8,128)S(1)} reduce(f32[2048,1,30]{2,1,0:T(1,128)S(1)} %bitcast.261, f32[]{:T(128)} %broadcast.68), dimensions={1}, to_apply=%bitcast.212.reduce_sub_computation | reduce | bytes 491524
  177.8 1.8 reshape.91
  179.6 3.4 %all-to-all-start.2 = ((f32[8,1,7680]{2,1,0:T(1,128)}), f32[8,1,7680]{2,1,0:T(1,128)S(1)}, u32[]{:S(2)}, u32[]{:S(2)}) async-start(f32[8,1,7680]{2,1,0:T(1,128)} %reshape.91), calls=%async_computation.2 | async-start | bytes 491520 | tf_op jit(solution)/shard_map/all_to_all | solution.py:104
  183.0 8.0 %all-to-all-done.2 = f32[8,1,7680]{2,1,0:T(1,128)S(1)} async-done(((f32[8,1,7680]{2,1,0:T(1,128)}), f32[8,1,7680]{2,1,0:T(1,128)S(1)}, u32[]{:S(2)}, u32[]{:S(2)}) %all-to-all-start.2) | async-done | bytes 245792 | tf_op jit(solution)/shard_map/all_to_all | solution.py:104
  192.3 1.9 reshape.92
  195.2 5.6 %while.92 = (s32[]{:T(128)}, f32[5,256]{1,0:T(8,128)S(1)}, f32[8,5,256]{2,1,0:T(8,128)}, f32[8,5,5,256]{3,0,2,1:T(8,128)S(1)}, f32[8,5,256]{2,0,1:T(8,128)S(1)}, /*index=5*/s32[]{:T(128)}, s32[]{:T(128)}, s32[]{:T(128)}) while((s32[]{:T(128)}, f32[5,256]{1,0:T(8,128)S(1)}, f32[8,5,256]{2,1,0:T(8,128)}, ...), condition=%wide.region_16.17_spmd.clone, body=%wide.region_14.16_spmd.clone.sunk | while | flops 14084 | bytes 131191 | solution.py:87
  200.8 3.4 %all-to-all-start.3 = ((f32[8,5,256]{2,1,0:T(8,128)}), f32[8,5,256]{2,1,0:T(8,128)S(1)}, u32[]{:S(2)}, u32[]{:S(2)}) async-start(f32[8,5,256]{2,1,0:T(8,128)} %get-tuple-element.448), calls=%async_computation.3 | async-start | bytes 131072 | tf_op jit(solution)/shard_map/all_to_all | solution.py:108
  205.1 5.9 %all-to-all-done.3 = f32[8,5,256]{2,1,0:T(8,128)S(1)} async-done(((f32[8,5,256]{2,1,0:T(8,128)}), f32[8,5,256]{2,1,0:T(8,128)S(1)}, u32[]{:S(2)}, u32[]{:S(2)}) %all-to-all-start.3) | async-done | bytes 40992 | tf_op jit(solution)/shard_map/all_to_all | solution.py:108
  211.1 44.0 %while.89 = (s32[]{:T(128)}, f32[5,16,128]{2,1,0:T(8,128)S(1)}, f32[16,5,16,128]{3,2,1,0:T(8,128)S(1)}, f32[16,5,16,128]{3,2,1,0:T(8,128)}, f32[16,5,5,16,128]{4...) while((s32[]{:T(128)}, f32[5,16,128]{2,1,0:T(8,128)S(1)}, ...), condition=%wide.region_19.20_spmd, body=%wide.region_17.19_spmd.sunk | while | flops 727043 | bytes 696529 | solution.py:178
  (580 shorter events, 152.7 us)
Async XLA Ops:
  0.6 8.8 %copy-start = (f32[5,5]{1,0:T(8,128)S(1)}, f32[5,5]{1,0:T(8,128)}, u32[]{:S(2)}) copy-start(f32[5,5]{1,0:T(8,128)} %param.30) | copy-start | bytes 304
  0.6 8.8 %copy-start.1 = (f32[16,5,16,128]{3,2,1,0:T(8,128)S(1)}, f32[16,5,16,128]{3,2,1,0:T(8,128)}, u32[]{:S(2)}) copy-start(f32[16,5,16,128]{3,2,1,0:T(8,128)} %param.23) | copy-start | bytes 1966084
  1.6 9.1 %copy-start.11 = (f32[16,16,128]{2,1,0:T(8,128)}, f32[16,16,128]{2,1,0:T(8,128)S(1)}, u32[]{:S(2)}) copy-start(f32[16,16,128]{2,1,0:T(8,128)S(1)} %convert_element_type.13) | copy-start | bytes 393220
  3.1 7.6 %copy-start.24 = (s32[16,16,128]{2,1,0:T(8,128)S(1)}, s32[16,16,128]{2,1,0:T(8,128)}, u32[]{:S(2)}) copy-start(s32[16,16,128]{2,1,0:T(8,128)} %param.27) | copy-start | bytes 393220
  3.1 8.4 %copy-start.26 = (f32[6,5,5]{2,0,1:T(8,128)S(1)}, f32[6,5,5]{2,0,1:T(8,128)}, u32[]{:S(2)}) copy-start(f32[6,5,5]{2,0,1:T(8,128)} %param.29) | copy-start | bytes 1804
  3.1 8.4 %copy-start.27 = (f32[5,5]{1,0:T(8,128)S(1)}, f32[5,5]{1,0:T(8,128)}, u32[]{:S(2)}) copy-start(f32[5,5]{1,0:T(8,128)} %param.28) | copy-start | bytes 304
  3.2 11.3 %collective-permute-start = (f32[1,5,16,128]{3,1,2,0:T(8,128)S(1)}, f32[1,5,16,128]{3,1,2,0:T(8,128)S(1)}, u32[]{:S(2)}, u32[]{:S(2)}) collective-permute-start(f32[1,5,16,128]{3,1,2,0:T(8,128)S(1)} %get-tuple-element.649), channel_id=1, source_target_pairs={{0,4},{4,8},{8,12},{12,16},{16,20},{20,24},{24,28},{1,5},{5,9},{9,... | collective-permute-start | bytes 122888 | tf_op jit(solution)/shard_map/ppermute | solution.py:12
  8.2 6.2 %collective-permute-start.1 = (f32[1,5,16,128]{3,1,2,0:T(8,128)S(1)}, f32[1,5,16,128]{3,1,2,0:T(8,128)S(1)}, u32[]{:S(2)}, u32[]{:S(2)}) collective-permute-start(f32[1,5,16,128]{3,1,2,0:T(8,128)S(1)} %get-tuple-element.650), channel_id=1, source_target_pairs={{4,0},{8,4},{12,8},{16,12},{20,16},{24,20},{28,24},{5,1},{9,5},{13... | collective-permute-start | bytes 122888 | tf_op jit(solution)/shard_map/ppermute | solution.py:15
  10.7 3.0 %copy-start.25 = (s32[16,16,128]{2,1,0:T(8,128)S(1)}, s32[16,16,128]{2,1,0:T(8,128)}, u32[]{:S(2)}) copy-start(s32[16,16,128]{2,1,0:T(8,128)} %param.26) | copy-start | bytes 393220
  14.4 9.7 %copy-start.6 = (f32[1,5,16,128]{3,1,2,0:T(8,128)}, f32[1,5,16,128]{3,1,2,0:T(8,128)S(1)}, u32[]{:S(2)}) copy-start(f32[1,5,16,128]{3,1,2,0:T(8,128)S(1)} %collective-permute-done.1) | copy-start | bytes 122884
  14.5 6.9 %collective-permute-start.2 = (f32[18,5,1,128]{3,1,2,0:T(8,128)S(1)}, f32[18,5,1,128]{3,1,2,0:T(8,128)S(1)}, u32[]{:S(2)}, u32[]{:S(2)}) collective-permute-start(f32[18,5,1,128]{3,1,2,0:T(8,128)S(1)} %get-tuple-element.647), channel_id=1, source_target_pairs={{0,2},{1,3},{4,6},{5,7},{8,10},{9,11},{12,14},{13,15},{16,18},{17,... | collective-permute-start | bytes 138248 | tf_op jit(solution)/shard_map/ppermute | solution.py:12
  17.9 6.2 %collective-permute-start.3 = (f32[18,5,1,128]{3,1,2,0:T(8,128)S(1)}, f32[18,5,1,128]{3,1,2,0:T(8,128)S(1)}, u32[]{:S(2)}, u32[]{:S(2)}) collective-permute-start(f32[18,5,1,128]{3,1,2,0:T(8,128)S(1)} %get-tuple-element.648), channel_id=1, source_target_pairs={{2,0},{3,1},{6,4},{7,5},{10,8},{11,9},{14,12},{15,13},{18,16},{19,... | collective-permute-start | bytes 138248 | tf_op jit(solution)/shard_map/ppermute | solution.py:15
  21.3 2.8 %copy-start.13 = (f32[18,5,1,128]{3,1,2,0:T(8,128)}, f32[18,5,1,128]{3,1,2,0:T(8,128)S(1)}, u32[]{:S(2)}) copy-start(f32[18,5,1,128]{3,1,2,0:T(8,128)S(1)} %collective-permute-done.2) | copy-start | bytes 138244
  28.9 9.9 %collective-permute-start.4 = (f32[18,5,18,1]{2,3,1,0:T(1,128)}, f32[18,5,18,1]{2,3,1,0:T(1,128)}, u32[]{:S(2)}, u32[]{:S(2)}) collective-permute-start(f32[18,5,18,1]{2,3,1,0:T(1,128)} %copy.207), channel_id=1, source_target_pairs={{0,1},{2,3},{4,5},{6,7},{8,9},{10,11},{12,13},{14,15},{16,17},{18,... | collective-permute-start | bytes 19448 | tf_op jit(solution)/shard_map/ppermute | solution.py:12
  32.1 9.5 %collective-permute-start.5 = (f32[18,5,18,1]{2,3,1,0:T(1,128)}, f32[18,5,18,1]{2,3,1,0:T(1,128)}, u32[]{:S(2)}, u32[]{:S(2)}) collective-permute-start(f32[18,5,18,1]{2,3,1,0:T(1,128)} %copy.210), channel_id=1, source_target_pairs={{1,0},{3,2},{5,4},{7,6},{9,8},{11,10},{13,12},{15,14},{17,16},{19,... | collective-permute-start | bytes 19448 | tf_op jit(solution)/shard_map/ppermute | solution.py:15
  33.6 3.1 %copy-start.7 = (f32[1,5,16,128]{3,1,2,0:T(8,128)S(1)}, f32[1,5,16,128]{3,1,2,0:T(8,128)}, u32[]{:S(2)}) copy-start(f32[1,5,16,128]{3,1,2,0:T(8,128)} %copy-done.6) | copy-start | bytes 122884
  33.6 3.1 %copy-start.14 = (f32[18,5,1,128]{3,1,2,0:T(8,128)S(1)}, f32[18,5,1,128]{3,1,2,0:T(8,128)}, u32[]{:S(2)}) copy-start(f32[18,5,1,128]{3,1,2,0:T(8,128)} %copy-done.13) | copy-start | bytes 138244
  33.6 3.1 %copy-start.23 = (pred[16,16,128]{2,1,0:T(8,128)(4,1)S(1)}, pred[16,16,128]{2,1,0:T(8,128)(4,1)}, u32[]{:S(2)}) copy-start(pred[16,16,128]{2,1,0:T(8,128)(4,1)} %get-tuple-element.653) | copy-start | bytes 98308
  43.4 2.7 %copy-start.8 = (f32[1,5,16,128]{3,1,2,0:T(8,128)S(1)}, f32[1,5,16,128]{3,1,2,0:T(8,128)}, u32[]{:S(2)}) copy-start(f32[1,5,16,128]{3,1,2,0:T(8,128)} %copy-done.6) | copy-start | bytes 122884
  43.4 2.7 %copy-start.15 = (f32[18,5,1,128]{3,1,2,0:T(8,128)S(1)}, f32[18,5,1,128]{3,1,2,0:T(8,128)}, u32[]{:S(2)}) copy-start(f32[18,5,1,128]{3,1,2,0:T(8,128)} %copy-done.13) | copy-start | bytes 138244
  43.4 2.7 %copy-start.17 = (f32[18,5,1,128]{3,1,2,0:T(8,128)S(1)}, f32[18,5,1,128]{3,1,2,0:T(8,128)}, u32[]{:S(2)}) copy-start(f32[18,5,1,128]{3,1,2,0:T(8,128)} %copy-done.16) | copy-start | bytes 138244
  43.4 2.7 %copy-start.22 = (pred[16,16,128]{2,1,0:T(8,128)(4,1)S(1)}, pred[16,16,128]{2,1,0:T(8,128)(4,1)}, u32[]{:S(2)}) copy-start(pred[16,16,128]{2,1,0:T(8,128)(4,1)} %get-tuple-element.655) | copy-start | bytes 98308
  43.4 4.3 %copy-start.10 = (f32[16,5,16,128]{3,2,1,0:T(8,128)S(1)}, f32[16,5,16,128]{3,2,1,0:T(8,128)}, u32[]{:S(2)}) copy-start(f32[16,5,16,128]{3,2,1,0:T(8,128)} %param.24) | copy-start | bytes 1966084
  46.1 1.8 copy-start.4
  46.1 2.1 copy-start.5
  46.1 2.1 copy-start.12
  46.1 2.2 copy-start.21
  83.8 16.6 %all-to-all-start = ((f32[8,1,30,256]{3,1,2,0:T(1,128)}), f32[8,1,30,256]{3,1,2,0:T(1,128)S(1)}, u32[]{:S(2)}, u32[]{:S(2)}) async-start(f32[8,1,30,256]{3,1,2,0:T(1,128)} %fusion.61), calls=%async_computation | async-start | bytes 491520 | tf_op jit(solution)/shard_map/all_to_all | solution.py:93
  106.8 10.8 %all-to-all-start.1 = ((f32[8,5,256]{2,1,0:T(8,128)}), f32[8,5,256]{2,1,0:T(8,128)S(1)}, u32[]{:S(2)}, u32[]{:S(2)}) async-start(f32[8,5,256]{2,1,0:T(8,128)} %get-tuple-element.444), calls=%async_computation.1 | async-start | bytes 131072 | tf_op jit(solution)/shard_map/all_to_all | solution.py:99
  117.7 19.4 %copy-start.19 = (f32[5,5]{1,0:T(8,128)S(1)}, f32[5,5]{1,0:T(8,128)}, u32[]{:S(2)}) copy-start(f32[5,5]{1,0:T(8,128)} %param.33) | copy-start | bytes 304
  179.6 11.5 %all-to-all-start.2 = ((f32[8,1,7680]{2,1,0:T(1,128)}), f32[8,1,7680]{2,1,0:T(1,128)S(1)}, u32[]{:S(2)}, u32[]{:S(2)}) async-start(f32[8,1,7680]{2,1,0:T(1,128)} %reshape.91), calls=%async_computation.2 | async-start | bytes 491520 | tf_op jit(solution)/shard_map/all_to_all | solution.py:104
  200.8 10.2 %all-to-all-start.3 = ((f32[8,5,256]{2,1,0:T(8,128)}), f32[8,5,256]{2,1,0:T(8,128)S(1)}, u32[]{:S(2)}, u32[]{:S(2)}) async-start(f32[8,5,256]{2,1,0:T(8,128)} %get-tuple-element.448), calls=%async_computation.3 | async-start | bytes 131072 | tf_op jit(solution)/shard_map/all_to_all | solution.py:108
  (6 other events, 7.4 us)
